TPU v7x, 32 devices: a whole 2x2x4 slice. The times are simulated.
32 devices in a mesh: groups: 2 (over y), ctx: 4 (over z), head: 2 (over x), rep: 2 (over core).
Axes of the slice: x: 2, y: 2, z: 4, core: 2. Of those that a mesh axis runs over, the one named last changes fastest.
Arguments:
- queries: bfloat16 [8192, 16, 2, 128], P(('groups', 'ctx'), 'head', 'rep'), parts along dimension 0, may hold values from -10 to 10
- keys_values: bfloat16 [2, 8192, 16, 128], P('rep', ('groups', 'ctx'), 'head'), parts along dimension 1, may hold values from -6 to 6
- far_list: int32 [64, 16], P('groups'), parts along dimension 0, may hold values from 0 to 31, as said below
- far_count: int32 [64], P('groups'), parts along dimension 0, may hold values from 0 to 8
Outputs:
- attended: bfloat16 [8192, 16, 2, 128], P(('groups', 'ctx'), 'head', 'rep'), parts along dimension 0
There are 2 independent parts, one for each index of `groups`. A program takes and returns all parts, laid end to end along the dimension named above; each array names one. Nothing has to cross between parts.
Inputs may be any that keep to these rules, and one draw needn't show every extreme that they name: `far_list`: for query block c, the entries j < far_count[c] are distinct block numbers no later than c - 4; entries from far_count[c] on are arbitrary and not read. Taken over all query blocks of one span of 1024 tokens, the counted entries name at most 2 distinct blocks of any one span, and some span's query blocks name exactly 2 of some span in every draw.
All inputs are finite; a program needn't handle non-finite values.
Results may differ from a plain program's by a relative error of at most 0.003.
Values may be sent and summed in bfloat16 or wider, within the bound.
A program may use at most 128 MiB of HBM per device.

v0:
```python
import jax
import jax.numpy as jnp
from jax import lax
from jax.sharding import PartitionSpec as P

BLK = 128
WB = 4
FSEL = 16
CAP = 2


floor_score = -1e30
score_scale = 1.0 / 12.0


def partner(block, axis, stride):
    count = lax.axis_size(axis)
    route = []
    for low in range(count):
        high = low | 1 << stride
        if high != low and high < count:
            route += [(low, high), (high, low)]
    return lax.ppermute(block, axis, route)


def from_behind(x, axis, by):
    count = lax.axis_size(axis)
    pairs = [(i, i + by) for i in range(count) if 0 <= i + by < count]
    return lax.ppermute(x, axis, pairs)


def group_weights(scores, usable):
    masked = jnp.where(usable, scores, floor_score)
    summit = jnp.max(masked, axis=-1, keepdims=True)
    weights = jnp.where(usable, jnp.exp(masked - summit), 0.0)
    return (summit, weights, jnp.sum(weights, axis=-1, keepdims=True))


def row_major(stacked):
    return jnp.moveaxis(stacked, 0, 2).reshape(
        stacked.shape[1], stacked.shape[2], stacked.shape[0] * stacked.shape[3], stacked.shape[-1]
    )


def local(queries, keys_values, far_list, far_count):
    tok_rows, head_count, query_group, head_width = queries.shape
    block_len = BLK
    own_blocks = tok_rows // block_len
    span_count = lax.axis_size("ctx")
    my_span = lax.axis_index("ctx")
    my_side = lax.axis_index("rep")
    rim_len = (WB - 1) * block_len
    rim_start = tok_rows - rim_len
    other_half = partner(keys_values, "rep", 0)
    local_pair = jnp.concatenate(
        [
            jnp.where(my_side == 0, keys_values, other_half),
            jnp.where(my_side == 0, other_half, keys_values),
        ],
        axis=0,
    )
    slot_range = jnp.arange(FSEL, dtype=jnp.int32)
    block_index = jnp.arange(own_blocks, dtype=jnp.int32)
    my_blocks = my_span * own_blocks + block_index
    counted = slot_range[None, :] < far_count[:, None]
    every_block = jnp.arange(span_count * own_blocks, dtype=jnp.int32)
    list_blocks = far_list.reshape(span_count, own_blocks, FSEL)
    counted_blocks = counted.reshape(span_count, own_blocks, FSEL)
    flat_lists = list_blocks.reshape(span_count, -1)
    flat_counted = counted_blocks.reshape(span_count, -1)
    wanted = jnp.any(
        (flat_lists[:, :, None] == my_blocks[None, None, :]) & flat_counted[:, :, None], axis=1
    )
    wanted_rank = jnp.cumsum(wanted.astype(jnp.int32), axis=1) - 1
    in_slot = wanted[:, None, :] & (
        wanted_rank[:, None, :] == jnp.arange(CAP, dtype=jnp.int32)[None, :, None]
    )
    send_index = jnp.sum(jnp.where(in_slot, block_index[None, None, :], 0), axis=2).reshape(-1)
    slot_width = CAP
    rim_pair = from_behind(local_pair[:, rim_start:], "ctx", 1)
    blocked = local_pair.reshape(local_pair.shape[0], own_blocks, block_len, head_count, head_width)
    pool_pair = lax.all_to_all(
        jnp.take(blocked, send_index, axis=1), "ctx", split_axis=1, concat_axis=1, tiled=True
    )
    my_list = lax.dynamic_slice_in_dim(far_list, my_span * own_blocks, own_blocks, 0)
    my_count = lax.dynamic_slice_in_dim(far_count, my_span * own_blocks, own_blocks, 0)
    my_counted = slot_range[None, :] < my_count[:, None]
    extended = jnp.concatenate([rim_pair, local_pair], axis=1)
    query_rows = min(4 * block_len, tok_rows)
    key_rows = query_rows + rim_len
    base_pos = my_span * tok_rows

    def near_part(first_row):
        query_tile = lax.dynamic_slice_in_dim(queries, first_row, query_rows, 0)
        pair_tile = lax.dynamic_slice_in_dim(extended, first_row, key_rows, 1)
        scores = (
            jnp.einsum(
                "qhgd,khd->hgqk", query_tile, pair_tile[0], preferred_element_type=jnp.float32
            )
            * score_scale
        )
        query_pos = first_row + jnp.arange(query_rows, dtype=jnp.int32)
        key_pos = first_row - rim_len + jnp.arange(key_rows, dtype=jnp.int32)
        usable = (
            (key_pos[None, :] <= query_pos[:, None])
            & (key_pos[None, :] // block_len >= query_pos[:, None] // block_len - WB + 1)
            & (base_pos + key_pos[None, :] >= 0)
        )
        summit, weights, weight_sum = group_weights(scores, usable)
        mixed_out = jnp.einsum(
            "hgqk,khd->hgqd",
            weights.astype(jnp.bfloat16),
            pair_tile[1],
            preferred_element_type=jnp.float32,
        )
        return (summit, mixed_out, weight_sum)

    starts = jnp.arange(tok_rows // query_rows, dtype=jnp.int32) * query_rows
    near_top, near_out, near_sum = lax.map(near_part, starts)
    far_keys_len = FSEL * block_len
    query_blocks = queries.reshape(own_blocks, block_len, head_count, query_group, head_width)
    named_block = (my_list.reshape(-1)[:, None] == every_block[None, :]) & my_counted.reshape(-1)[
        :, None
    ]
    needed = jnp.any(named_block, axis=0).reshape(span_count, own_blocks)
    place = (
        jnp.cumsum(needed.astype(jnp.int32), axis=1)
        - 1
        + 0
        + jnp.arange(span_count, dtype=jnp.int32)[:, None] * slot_width
    )
    own_slots = jnp.sum(jnp.where(named_block, place.reshape(-1)[None, :], 0), axis=1).reshape(
        my_list.shape[0], FSEL
    )
    total = query_blocks.shape[0]
    width_step = 4
    turns = total // width_step

    def far_group(task):
        query_tile, slot_tile, live = task
        keys_tile = jnp.take(pool_pair[0], slot_tile.reshape(-1), axis=0).reshape(
            width_step, far_keys_len, head_count, head_width
        )
        value_tile = jnp.take(pool_pair[1], slot_tile.reshape(-1), axis=0).reshape(
            width_step, far_keys_len, head_count, head_width
        )
        scores = (
            jnp.einsum(
                "bqhgd,bkhd->bhgqk", query_tile, keys_tile, preferred_element_type=jnp.float32
            )
            * score_scale
        )
        usable = jnp.repeat(slot_range[None, :] < live[:, None], block_len, axis=1)[
            :, None, None, None, :
        ]
        summit, weights, weight_sum = group_weights(scores, usable)
        mixed_out = jnp.einsum(
            "bhgqk,bkhd->bhgqd",
            weights.astype(jnp.bfloat16),
            value_tile,
            preferred_element_type=jnp.float32,
        )
        return (summit, mixed_out, weight_sum)

    grouped = (
        query_blocks.reshape((turns, width_step) + query_blocks.shape[1:]),
        own_slots.reshape(turns, width_step, FSEL),
        my_count.reshape(turns, width_step),
    )
    results = lax.map(far_group, grouped)
    own_top, own_out, own_sum = tuple(
        (piece.reshape((total,) + piece.shape[2:]) for piece in results)
    )
    far_top, far_out, far_sum = (row_major(own_top), row_major(own_out), row_major(own_sum))
    near_top, near_out, near_sum = (row_major(near_top), row_major(near_out), row_major(near_sum))
    summit = jnp.maximum(near_top, far_top)
    near_scale = jnp.exp(near_top - summit)
    far_scale = jnp.exp(far_top - summit)
    result = (near_scale * near_out + far_scale * far_out) / (
        near_scale * near_sum + far_scale * far_sum
    )
    return jnp.transpose(result, (2, 0, 1, 3)).astype(jnp.bfloat16)


def solution(mesh):
    in_specs = (
        P(("groups", "ctx"), "head", "rep", None),
        P("rep", ("groups", "ctx"), "head", None),
        P("groups", None),
        P("groups"),
    )
    out_specs = P(("groups", "ctx"), "head", "rep", None)
    return jax.shard_map(local, mesh=mesh, in_specs=in_specs, out_specs=out_specs, check_vma=False)
```

profile of v0, /device:TPU:17, one launch (start us, length us, event | category | flops | bytes accessed | tf_op | source)
XLA Modules:
  0.0 354.4 jit_solution(871911679812161485)
XLA Ops:
  19.3 4.6 %copy.52 = bf16[2,1024,8,128]{3,2,1,0:T(8,128)(2,1)} copy(bf16[2,1024,8,128]{3,1,2,0:T(8,128)(2,1)S(1)} %pad_maximum_fusion) | data formatting | bytes 8388608 | tf_op jit(solution)/shard_map/concatenate | solution.py:55
  23.9 5.2 %gather_fusion.2 = bf16[8,2,128,8,128]{4,3,2,1,0:T(8,128)(2,1)} fusion(bf16[2,8,128,8,128]{4,3,2,1,0:T(8,128)(2,1)} %bitcast.197, s32[1024]{0:T(1024)S(1)} %pad_clamp_fusion.1), kind=kCustom, calls=%fused_computation.2 | custom fusion | bytes 8388640 | tf_op jit(solution)/shard_map/jit(_take)/gather | solution.py:83
  29.2 4.6 %select_bitcast_fusion = bf16[2,8,128,8,128]{4,3,2,0,1:T(8,128)(2,1)} fusion(bf16[8,2,128,8,128]{4,3,2,1,0:T(8,128)(2,1)} %gather_fusion.2, pred[8]{0:T(512)(128)(4,1)S(1)} %compare_and_fusion.1), kind=kLoop, calls=%fused_computation.88 | loop fusion | flops 2097152 | bytes 8388616 | tf_op jit(solution)/shard_map/jit(_take)/select_n | solution.py:83
  33.8 6.0 %all-to-all-start = ((bf16[2,8,128,8,128]{4,3,2,0,1:T(8,128)(2,1)}), bf16[2,8,128,8,128]{4,3,2,0,1:T(8,128)(2,1)}, u32[]{:S(2)}, u32[]{:S(2)}) async-start(bf16[2,8,128,8,128]{4,3,2,0,1:T(8,128)(2,1)} %select_bitcast_fusion), calls=%async_computation | async-start | bytes 8388608 | tf_op jit(solution)/shard_map/all_to_all | solution.py:82
  39.8 11.4 %collective-permute-done.1 = bf16[2,384,8,128]{3,1,2,0:T(8,128)(2,1)} collective-permute-done((bf16[2,384,8,128]{3,1,2,0:T(8,128)(2,1)}, bf16[2,384,8,128]{3,1,2,0:T(8,128)(2,1)}, u32[]{:S(2)}, u32[]{:S(2)}) %collective-permute-start.1) | collective-permute-done | bytes 1572896 | tf_op jit(solution)/shard_map/ppermute | solution.py:29
  51.3 4.9 %maximum_maximum_fusion = bf16[2,1408,8,128]{3,1,2,0:T(8,128)(2,1)} fusion(bf16[1,1024,8,128]{3,1,2,0:T(8,128)(2,1)} %copy-done.1, bf16[1,1024,8,128]{3,1,2,0:T(8,128)(2,1)S(1)} %get-tuple-element.367, bf16[2,384,8,128]{3,1,2,0:T(8,128)(2,1)} %collective-permute-done.1), kind=kLoop, calls=%fused_computation.84 | loop fusion | flops 17301504 | bytes 11534336 | tf_op jit(solution)/shard_map/concatenate | solution.py:88
  56.2 72.9 %while.34 = (s32[]{:T(128)}, f32[2,8,1,512,1]{3,1,4,2,0:T(8,128)S(1)}, f32[2,8,1,512,128]{4,3,1,2,0:T(8,128)}, f32[2,8,1,512,1]{3,4,2,1,0:T(1,128)S(1)}, s32[2]{...) while((s32[]{:T(128)}, ...), condition=%wide.region_3.4_spmd, body=%wide.region_0.3_spmd.sunk | while | flops 1928610944 | bytes 54944268 | solution.py:119
  63.5 8.4 %fusion.67 = (f32[8,512]{1,0:T(8,128)S(1)}, f32[8,896,512]{2,1,0:T(8,128)}) fusion(pred[512,896]{0,1:T(8,128)(4,1)S(1)} %and_and_fusion.2, bf16[512,8,1,128]{3,1,2,0:T(8,128)(2,1)S(1)} %constant_dynamic-slice_fusion.8, bf16[2,1408,8,128]{3,1,2,0:T(8,128)(2,1)} %get-tuple-element.552, s32[]{:T(128)S(6)} %select_n.250), kind=kOutput, calls=%fused_computation.6.clone.1 | convolution fusion | flops 950530048 | bytes 18038788 | tf_op jit(solution)/shard_map/while/body/eval_jaxpr/qhgd,khd->hgqk/dot_general | solution.py:97
  71.9 8.7 %fusion.68 = f32[8,512]{1,0:T(8,128)S(1)} fusion(f32[8,896,512]{2,1,0:T(8,128)} %get-tuple-element.476, f32[8,512]{1,0:T(8,128)S(1)} %get-tuple-element.475, pred[512,896]{0,1:T(8,128)(4,1)S(1)} %and_and_fusion.2), kind=kLoop, calls=%fused_computation.7.clone.1 | loop fusion | flops 18345984 | bytes 15171584 | tf_op jit(solution)/shard_map/while/body/eval_jaxpr/reduce_sum | solution.py:36
  80.6 12.1 %bitcast_dynamic-update-slice_fusion.9 = f32[2,8,1,512,128]{4,3,1,2,0:T(8,128)} fusion(f32[2,8,1,512,128]{4,3,1,2,0:T(8,128)} %get-tuple-element.534, s32[]{:T(128)} %get-tuple-element.532, bf16[2,1408,8,128]{3,1,2,0:T(8,128)(2,1)} %get-tuple-element.552, s32[]{:T(128)S(6)} %add.369, s32[]{:T(128)S(6)} %select_n.250, ...), kind=kOutput, calls=%fused_computation.12.clone.1 | convolution fusion | flops 957874176 | bytes 19087880 | tf_op jit(solution)/shard_map/while/body/eval_jaxpr/hgqk,khd->hgqd/dot_general | solution.py:110
  100.0 8.4 %fusion.67 = (f32[8,512]{1,0:T(8,128)S(1)}, f32[8,896,512]{2,1,0:T(8,128)}) fusion(pred[512,896]{0,1:T(8,128)(4,1)S(1)} %and_and_fusion.2, bf16[512,8,1,128]{3,1,2,0:T(8,128)(2,1)S(1)} %constant_dynamic-slice_fusion.8, bf16[2,1408,8,128]{3,1,2,0:T(8,128)(2,1)} %get-tuple-element.552, s32[]{:T(128)S(6)} %select_n.250), kind=kOutput, calls=%fused_computation.6.clone.1 | convolution fusion | flops 950530048 | bytes 18038788 | tf_op jit(solution)/shard_map/while/body/eval_jaxpr/qhgd,khd->hgqk/dot_general | solution.py:97
  108.4 8.7 %fusion.68 = f32[8,512]{1,0:T(8,128)S(1)} fusion(f32[8,896,512]{2,1,0:T(8,128)} %get-tuple-element.476, f32[8,512]{1,0:T(8,128)S(1)} %get-tuple-element.475, pred[512,896]{0,1:T(8,128)(4,1)S(1)} %and_and_fusion.2), kind=kLoop, calls=%fused_computation.7.clone.1 | loop fusion | flops 18345984 | bytes 15171584 | tf_op jit(solution)/shard_map/while/body/eval_jaxpr/reduce_sum | solution.py:36
  117.1 12.0 %bitcast_dynamic-update-slice_fusion.9 = f32[2,8,1,512,128]{4,3,1,2,0:T(8,128)} fusion(f32[2,8,1,512,128]{4,3,1,2,0:T(8,128)} %get-tuple-element.534, s32[]{:T(128)} %get-tuple-element.532, bf16[2,1408,8,128]{3,1,2,0:T(8,128)(2,1)} %get-tuple-element.552, s32[]{:T(128)S(6)} %add.369, s32[]{:T(128)S(6)} %select_n.250, ...), kind=kOutput, calls=%fused_computation.12.clone.1 | convolution fusion | flops 957874176 | bytes 19087880 | tf_op jit(solution)/shard_map/while/body/eval_jaxpr/hgqk,khd->hgqd/dot_general | solution.py:110
  129.8 6.5 %copy.59 = f32[8,1,2,512,128]{4,0,3,2,1:T(8,128)} copy(f32[8,1,2,512,128]{4,3,0,1,2:T(8,128)} %bitcast.198) | data formatting | bytes 8388608 | tf_op jit(solution)/shard_map/transpose | solution.py:40
  136.3 4.6 %copy.56 = bf16[2,8,128,8,128]{4,3,2,1,0:T(8,128)(2,1)} copy(bf16[2,8,128,8,128]{4,3,2,0,1:T(8,128)(2,1)} %all-to-all-done) | data formatting | bytes 8388608
  140.9 202.4 %while.35 = (s32[]{:T(128)}, f32[2,4,8,1,128,1]{4,2,1,5,3,0:T(8,128)S(1)}, f32[2,4,8,1,128,128]{5,4,2,1,3,0:T(8,128)}, f32[2,4,8,1,128,1]{4,5,3,2,1,0:T(1,128)S(...) while((s32[]{:T(128)}, ...), condition=%wide.region_13.15_spmd.clone, body=%wide.region_10.14_spmd.clone.sunk | while | flops 4420789760 | bytes 290651552 | solution.py:170
  141.0 3.9 %slice_bitcast_fusion.3 = (bf16[8,128,8,128]{3,2,1,0:T(8,128)(2,1)}, bf16[8,128,8,128]{3,2,1,0:T(8,128)(2,1)S(1)}) fusion(bf16[2,8,128,8,128]{4,3,2,1,0:T(8,128)(2,1)} %get-tuple-element.514), kind=kLoop, calls=%fused_computation.66.clone.1 | loop fusion | bytes 8388608 | tf_op jit(solution)/shard_map/while/body/eval_jaxpr/squeeze | solution.py:144
  144.9 8.8 %gather_fusion = bf16[64,128,8,128]{3,2,1,0:T(8,128)(2,1)} fusion(bf16[8,128,8,128]{3,2,1,0:T(8,128)(2,1)} %get-tuple-element.485, s32[1024]{0:T(1024)S(1)} %pad_clamp_fusion.3), kind=kCustom, calls=%fused_computation.1.clone.clone.1 | custom fusion | bytes 33554688 | tf_op jit(solution)/shard_map/while/body/eval_jaxpr/jit(_take)/gather | solution.py:144
  153.8 7.3 %gather_fusion.1 = bf16[64,128,8,128]{3,2,1,0:T(8,128)(2,1)} fusion(bf16[8,128,8,128]{3,2,1,0:T(8,128)(2,1)S(1)} %get-tuple-element.486, s32[1024]{0:T(1024)S(1)} %pad_clamp_fusion.3), kind=kCustom, calls=%fused_computation.clone.clone.1 | custom fusion | bytes 33554688 | tf_op jit(solution)/shard_map/while/body/eval_jaxpr/jit(_take)/gather | solution.py:141
  161.0 23.2 %broadcast_select_fusion.5 = (bf16[64,128,8,128]{3,2,1,0:T(8,128)(2,1)}, bf16[64,128,8,128]{3,2,1,0:T(8,128)(2,1)}) fusion(bf16[64,128,8,128]{3,2,1,0:T(8,128)(2,1)} %gather_fusion, pred[64]{0:T(512)(128)(4,1)S(1)} %compare_and_fusion.3, bf16[64,128,8,128]{3,2,1,0:T(8,128)(2,1)} %gather_fusion.1), kind=kLoop, calls=%fused_computation.61.clone.1 | loop fusion | flops 16777216 | bytes 67108928 | tf_op jit(solution)/shard_map/while/body/eval_jaxpr/jit(_take)/select_n | solution.py:144
  184.5 19.7 %bitcast_reduce_fusion.2 = (f32[4,8,128]{2,1,0:T(8,128)S(1)}, f32[4,8,2048,128]{3,2,1,0:T(8,128)}) fusion(pred[4,2048]{1,0:T(4,128)(4,1)S(1)} %bitcast.199, bf16[1,4,128,8,1,128]{5,3,2,1,0,4:T(8,128)(2,1)S(1)} %constant_dynamic-slice_fusion.9, bf16[4,2048,8,128]{3,2,1,0:T(8,128)(2,1)} %bitcast.193), kind=kOutput, calls=%fused_computation.47.clone.1 | convolution fusion | flops 2172645376 | bytes 51404800 | tf_op jit(solution)/shard_map/while/body/eval_jaxpr/bqhgd,bkhd->bhgqk/dot_general | solution.py:148
  204.2 15.1 %fusion.72 = f32[4,8,128]{2,1,0:T(8,128)S(1)} fusion(f32[4,8,2048,128]{3,2,1,0:T(8,128)} %get-tuple-element.490, f32[4,8,128]{2,1,0:T(8,128)S(1)} %get-tuple-element.488, pred[4,2048]{1,0:T(4,128)(4,1)S(1)} %bitcast.200), kind=kLoop, calls=%fused_computation.51.clone.1 | loop fusion | flops 41938944 | bytes 33595392 | tf_op jit(solution)/shard_map/while/body/eval_jaxpr/reduce_sum | solution.py:36
  219.4 22.7 %bitcast_dynamic-update-slice_fusion.11 = f32[2,4,8,1,128,128]{5,4,2,1,3,0:T(8,128)} fusion(f32[2,4,8,1,128,128]{5,4,2,1,3,0:T(8,128)} %get-tuple-element.502, s32[]{:T(128)} %get-tuple-element.500, bf16[4,2048,8,128]{3,2,1,0:T(8,128)(2,1)} %bitcast.192, f32[4,8,2048,128]{3,2,1,0:T(8,128)} %get-tuple-element.490, ...), kind=kOutput, calls=%fused_computation.65.clone.1 | convolution fusion | flops 2189426688 | bytes 52462080 | tf_op jit(solution)/shard_map/while/body/eval_jaxpr/bhgqk,bkhd->bhgqd/dot_general | solution.py:157
  242.2 3.9 %slice_bitcast_fusion.3 = (bf16[8,128,8,128]{3,2,1,0:T(8,128)(2,1)}, bf16[8,128,8,128]{3,2,1,0:T(8,128)(2,1)S(1)}) fusion(bf16[2,8,128,8,128]{4,3,2,1,0:T(8,128)(2,1)} %get-tuple-element.514), kind=kLoop, calls=%fused_computation.66.clone.1 | loop fusion | bytes 8388608 | tf_op jit(solution)/shard_map/while/body/eval_jaxpr/squeeze | solution.py:144
  246.1 8.9 %gather_fusion = bf16[64,128,8,128]{3,2,1,0:T(8,128)(2,1)} fusion(bf16[8,128,8,128]{3,2,1,0:T(8,128)(2,1)} %get-tuple-element.485, s32[1024]{0:T(1024)S(1)} %pad_clamp_fusion.3), kind=kCustom, calls=%fused_computation.1.clone.clone.1 | custom fusion | bytes 33554688 | tf_op jit(solution)/shard_map/while/body/eval_jaxpr/jit(_take)/gather | solution.py:144
  254.9 7.3 %gather_fusion.1 = bf16[64,128,8,128]{3,2,1,0:T(8,128)(2,1)} fusion(bf16[8,128,8,128]{3,2,1,0:T(8,128)(2,1)S(1)} %get-tuple-element.486, s32[1024]{0:T(1024)S(1)} %pad_clamp_fusion.3), kind=kCustom, calls=%fused_computation.clone.clone.1 | custom fusion | bytes 33554688 | tf_op jit(solution)/shard_map/while/body/eval_jaxpr/jit(_take)/gather | solution.py:141
  262.2 23.2 %broadcast_select_fusion.5 = (bf16[64,128,8,128]{3,2,1,0:T(8,128)(2,1)}, bf16[64,128,8,128]{3,2,1,0:T(8,128)(2,1)}) fusion(bf16[64,128,8,128]{3,2,1,0:T(8,128)(2,1)} %gather_fusion, pred[64]{0:T(512)(128)(4,1)S(1)} %compare_and_fusion.3, bf16[64,128,8,128]{3,2,1,0:T(8,128)(2,1)} %gather_fusion.1), kind=kLoop, calls=%fused_computation.61.clone.1 | loop fusion | flops 16777216 | bytes 67108928 | tf_op jit(solution)/shard_map/while/body/eval_jaxpr/jit(_take)/select_n | solution.py:144
  285.7 19.7 %bitcast_reduce_fusion.2 = (f32[4,8,128]{2,1,0:T(8,128)S(1)}, f32[4,8,2048,128]{3,2,1,0:T(8,128)}) fusion(pred[4,2048]{1,0:T(4,128)(4,1)S(1)} %bitcast.199, bf16[1,4,128,8,1,128]{5,3,2,1,0,4:T(8,128)(2,1)S(1)} %constant_dynamic-slice_fusion.9, bf16[4,2048,8,128]{3,2,1,0:T(8,128)(2,1)} %bitcast.193), kind=kOutput, calls=%fused_computation.47.clone.1 | convolution fusion | flops 2172645376 | bytes 51404800 | tf_op jit(solution)/shard_map/while/body/eval_jaxpr/bqhgd,bkhd->bhgqk/dot_general | solution.py:148
  305.4 15.1 %fusion.72 = f32[4,8,128]{2,1,0:T(8,128)S(1)} fusion(f32[4,8,2048,128]{3,2,1,0:T(8,128)} %get-tuple-element.490, f32[4,8,128]{2,1,0:T(8,128)S(1)} %get-tuple-element.488, pred[4,2048]{1,0:T(4,128)(4,1)S(1)} %bitcast.200), kind=kLoop, calls=%fused_computation.51.clone.1 | loop fusion | flops 41938944 | bytes 33595392 | tf_op jit(solution)/shard_map/while/body/eval_jaxpr/reduce_sum | solution.py:36
  320.6 22.7 %bitcast_dynamic-update-slice_fusion.11 = f32[2,4,8,1,128,128]{5,4,2,1,3,0:T(8,128)} fusion(f32[2,4,8,1,128,128]{5,4,2,1,3,0:T(8,128)} %get-tuple-element.502, s32[]{:T(128)} %get-tuple-element.500, bf16[4,2048,8,128]{3,2,1,0:T(8,128)(2,1)} %bitcast.192, f32[4,8,2048,128]{3,2,1,0:T(8,128)} %get-tuple-element.490, ...), kind=kOutput, calls=%fused_computation.65.clone.1 | convolution fusion | flops 2189426688 | bytes 52462080 | tf_op jit(solution)/shard_map/while/body/eval_jaxpr/bhgqk,bkhd->bhgqd/dot_general | solution.py:157
  343.9 4.7 %copy.61 = f32[8,8,1,128,128]{4,1,3,0,2:T(8,128)S(1)} copy(f32[8,8,1,128,128]{4,3,1,0,2:T(8,128)} %bitcast.24) | data formatting | bytes 8388608 | tf_op jit(solution)/shard_map/reshape | solution.py:172
  348.7 5.8 %fusion.47 = bf16[1024,8,1,128]{3,1,2,0:T(8,128)(2,1)} fusion(f32[8,1024]{0,1:T(8,128)S(1)} %copy.63, f32[8,1,1024,128]{3,0,1,2:T(8,128)S(1)} %bitcast.196, f32[8,1024]{0,1:T(8,128)S(1)} %copy.60, f32[8,1,1024,128]{3,0,1,2:T(8,128)S(1)} %bitcast.195, f32[8,1024]{0,1:T(8,128)S(1)} %copy.58), kind=kLoop, calls=%fused_computation.90 | loop fusion | flops 5242880 | bytes 10584064 | tf_op jit(solution)/shard_map/convert_element_type | solution.py:182
  (115 shorter events, 28.2 us)
Async XLA Ops:
  1.9 5.8 %collective-permute-start = (bf16[1,1024,8,128]{3,1,2,0:T(8,128)(2,1)S(1)}, bf16[1,1024,8,128]{3,1,2,0:T(8,128)(2,1)}, u32[]{:S(2)}, u32[]{:S(2)}) collective-permute-start(bf16[1,1024,8,128]{3,1,2,0:T(8,128)(2,1)S(1)} %copy.46), channel_id=1, source_target_pairs={{0,1},{1,0},{2,3},{3,2},{4,5},{5,4},{6,7},{7,6},{8,9},{9,8},{10,11... | collective-permute-start | bytes 6291464 | tf_op jit(solution)/shard_map/ppermute | solution.py:23
  10.5 1.3 copy-start.1
  13.1 38.1 %collective-permute-start.1 = (bf16[2,384,8,128]{3,1,2,0:T(8,128)(2,1)}, bf16[2,384,8,128]{3,1,2,0:T(8,128)(2,1)}, u32[]{:S(2)}, u32[]{:S(2)}) collective-permute-start(bf16[2,384,8,128]{3,1,2,0:T(8,128)(2,1)} %fusion.48), channel_id=1, source_target_pairs={{0,4},{4,8},{8,12},{1,5},{5,9},{9,13},{2,6},{6,10},{10,14},{3,7},{... | collective-permute-start | bytes 4718600 | tf_op jit(solution)/shard_map/ppermute | solution.py:29
  16.7 0.6 copy-start.3
  33.8 102.5 %all-to-all-start = ((bf16[2,8,128,8,128]{4,3,2,0,1:T(8,128)(2,1)}), bf16[2,8,128,8,128]{4,3,2,0,1:T(8,128)(2,1)}, u32[]{:S(2)}, u32[]{:S(2)}) async-start(bf16[2,8,128,8,128]{4,3,2,0,1:T(8,128)(2,1)} %select_bitcast_fusion), calls=%async_computation | async-start | bytes 8388608 | tf_op jit(solution)/shard_map/all_to_all | solution.py:82
  129.1 11.8 %copy-start.6 = (f32[2,8,1,512,1]{3,1,4,2,0:T(8,128)}, f32[2,8,1,512,1]{3,1,4,2,0:T(8,128)S(1)}, u32[]{:S(2)}) copy-start(f32[2,8,1,512,1]{3,1,4,2,0:T(8,128)S(1)} %get-tuple-element.248) | copy-start | bytes 98308
  136.3 4.6 %copy-start.4 = (f32[2,4,8,1,128,1]{4,2,1,5,3,0:T(8,128)S(1)}, f32[2,4,8,1,128,1]{4,2,1,5,3,0:T(8,128)}, u32[]{:S(2)}) copy-start(f32[2,4,8,1,128,1]{4,2,1,5,3,0:T(8,128)} %copy-done.3) | copy-start | bytes 98308
  140.9 202.4 %copy-start.5 = (f32[1,8,2,512]{3,1,2,0:T(8,128)S(1)}, f32[1,8,2,512]{3,1,2,0:T(8,128)}, u32[]{:S(2)}) copy-start(f32[1,8,2,512]{3,1,2,0:T(8,128)} %copy.69) | copy-start | bytes 98308
  140.9 202.4 %copy-start.7 = (f32[2,8,1,512,1]{3,1,4,2,0:T(8,128)S(1)}, f32[2,8,1,512,1]{3,1,4,2,0:T(8,128)}, u32[]{:S(2)}) copy-start(f32[2,8,1,512,1]{3,1,4,2,0:T(8,128)} %copy-done.6) | copy-start | bytes 98308
  161.0 23.4 %copy-start = (bf16[2,4,128,8,1,128]{5,3,2,1,0,4:T(8,128)(2,1)S(1)}, bf16[2,4,128,8,1,128]{5,3,2,1,0,4:T(8,128)(2,1)}, u32[]{:S(2)}) copy-start(bf16[2,4,128,8,1,128]{5,3,2,1,0,4:T(8,128)(2,1)} %get-tuple-element.516) | copy-start | bytes 6291460 | tf_op jit(solution)/shard_map/while
  262.2 23.4 %copy-start = (bf16[2,4,128,8,1,128]{5,3,2,1,0,4:T(8,128)(2,1)S(1)}, bf16[2,4,128,8,1,128]{5,3,2,1,0,4:T(8,128)(2,1)}, u32[]{:S(2)}) copy-start(bf16[2,4,128,8,1,128]{5,3,2,1,0,4:T(8,128)(2,1)} %get-tuple-element.516) | copy-start | bytes 6291460 | tf_op jit(solution)/shard_map/while
  343.9 4.7 %copy-start.2 = (f32[8,1,2,512,128]{4,0,3,2,1:T(8,128)S(1)}, f32[8,1,2,512,128]{4,0,3,2,1:T(8,128)}, u32[]{:S(2)}) copy-start(f32[8,1,2,512,128]{4,0,3,2,1:T(8,128)} %copy.59) | copy-start | bytes 12582916
where the time goes:
time: 361 us; the launch traced here: 354 us
  matrix products  126 us (35%)
  other arithmetic  120 us (33%)
  local copies, waits for them, and re-layouts  79.4 us (22%)
  waiting for transfers between devices  11.4 us (3%)
  starting transfers between devices  9.94 us (3%)
  loops' own time  7.96 us (2%)
    reduce_sum x4, other arithmetic, group_weights(): return (summit, weights, jnp.sum(weights, axis=-1, keepdims=True))  47.6 us
    select_n x2, other arithmetic, far_group(): jnp.take(pool_pair[1], slot_tile.reshape(-1), axis=0)  46.4 us
    dot_general x2, matrix products, far_group(): jnp.einsum('bhgqk,bkhd->bhgqd', weights.astype(jnp.bfloat16), value_tile,...  45.4 us
    dot_general x2, matrix products, far_group(): jnp.einsum('bqhgd,bkhd->bhgqk', query_tile, keys_tile, preferred_element_...  39.4 us
    dot_general x2, matrix products, near_part(): jnp.einsum('hgqk,khd->hgqd', weights.astype(jnp.bfloat16), pair_tile[1],...  24 us
    gather x2, local copies, waits for them, and re-layouts, far_group(): jnp.take(pool_pair[1], slot_tile.reshape(-1), axis=0)  17.7 us
    dot_general x2, matrix products, near_part(): jnp.einsum('qhgd,khd->hgqk', query_tile, pair_tile[0], preferred_element_...  16.8 us
    gather x2, local copies, waits for them, and re-layouts, far_group(): jnp.take(pool_pair[0], slot_tile.reshape(-1), axis=0)  14.5 us
  transfers between devices with their start and end apart: 3, of which 1 were waited for; matrix products, arithmetic and copies ran while one was open for 28% of the time, Pallas kernels for 0%

commit v1 on v0

v1 whole, which is shorter than its diff:
```python
import functools
import math

import jax
import jax.numpy as jnp
from jax import lax
from jax.experimental import pallas as pl
from jax.experimental.pallas import tpu as pltpu
from jax.sharding import PartitionSpec as P

BLK = 128
WB = 4
FSEL = 16
CAP = 2

LANES = 128
MASKED = -1e30
SCALE = math.log2(math.e) / 12.0
NT = (((1,), (1,)), ((), ()))


def kernel(
    spans, listed, q_in, kv_in, out,
    q_raw, mine, loc, rim, far, sendbuf, qh, kh, vh, tk, tv, acc, top, bias, scr, o_raw,
    in_sem, x_send, x_recv, rz_send, rz_recv, rf_send, rf_recv,
    fz_send, fz_recv, ff_send, ff_recv, out_sem,
):
    toks, heads, dh = q_in.shape
    own = toks // BLK
    me = lax.axis_index("ctx")
    side = lax.axis_index("rep")
    mate = {"rep": 1 - side}
    rims = WB - 1

    load_kv = pltpu.make_async_copy(kv_in.at[0], mine, in_sem.at[0])
    load_loc = pltpu.make_async_copy(kv_in.at[0], loc.at[side], in_sem.at[2])
    load_q = pltpu.make_async_copy(q_in, q_raw, in_sem.at[1])
    load_kv.start()
    load_q.start()
    load_loc.start()

    barrier = pltpu.get_barrier_semaphore()
    pl.semaphore_signal(barrier, inc=1, device_id=mate)

    def greet(i, _):
        pl.semaphore_signal(barrier, inc=1, device_id={"ctx": lax.rem(me + i, spans)})
        return 0

    lax.fori_loop(1, spans, greet, 0)
    pl.semaphore_wait(barrier, spans)

    def rim_copy(j, to):
        return pltpu.make_async_remote_copy(
            src_ref=kv_in.at[0, own - j],
            dst_ref=rim.at[side, j - 1],
            send_sem=rz_send.at[j - 1], recv_sem=rz_recv.at[j - 1],
            device_id={"ctx": to},
        )

    def rim_pass(j):
        return pltpu.make_async_remote_copy(
            src_ref=rim.at[side, j - 1], dst_ref=rim.at[side, j - 1],
            send_sem=rf_send.at[j - 1], recv_sem=rf_recv.at[j - 1],
            device_id=mate,
        )

    def far_copy(to):
        return pltpu.make_async_remote_copy(
            src_ref=sendbuf.at[to], dst_ref=far.at[side, me],
            send_sem=fz_send.at[to], recv_sem=fz_recv.at[me],
            device_id={"ctx": to},
        )

    def far_arrival(src):
        return pltpu.make_async_remote_copy(
            src_ref=sendbuf.at[src], dst_ref=far.at[side, src],
            send_sem=fz_send.at[src], recv_sem=fz_recv.at[src],
            device_id={"ctx": src},
        )

    def far_pass(src):
        return pltpu.make_async_remote_copy(
            src_ref=far.at[side, src], dst_ref=far.at[side, src],
            send_sem=ff_send.at[src], recv_sem=ff_recv.at[src],
            device_id=mate,
        )

    ahead = lax.rem(me + 1, spans)
    has_next = me + 1 < spans

    @pl.when(has_next)
    def _():
        rim_copy(1, ahead).start()

    swap = pltpu.make_async_remote_copy(
        src_ref=kv_in.at[0], dst_ref=loc.at[side],
        send_sem=x_send, recv_sem=x_recv, device_id=mate,
    )
    swap.start()

    big = jnp.int32(1 << 30)

    def slots(dst, src):
        lists = listed[pl.ds(pl.multiple_of(dst * own, own), own), :]
        inside = (lists >= src * own) & (lists < src * own + own)
        first = jnp.min(jnp.where(inside, lists, big))
        second = jnp.min(jnp.where(inside & (lists > first), lists, big))
        return lists, (first, second)

    def local_row(block):
        row = jnp.where(block < big, block - me * own, 0)
        return jnp.clip(row, 0, own - 1)

    load_kv.wait()

    def fill(i, _):
        to = spans - 1 - i
        _, found = slots(to, me)
        for k in range(CAP):
            sendbuf[to, k] = mine[local_row(found[k])]
        return 0

    later = spans - 1 - me
    lax.fori_loop(0, later, fill, 0)

    def push(i, _):
        far_copy(spans - 1 - i).start()
        return 0

    lax.fori_loop(0, later, push, 0)

    @pl.when(has_next)
    def _():
        for j in range(2, WB):
            rim_copy(j, ahead).start()

    def spread(block, put):
        scr[...] = block.astype(jnp.float32).reshape(BLK * heads, dh)
        for h in range(heads):
            put(h, scr[pl.ds(h, BLK, stride=heads), :].astype(jnp.bfloat16))

    tv[:, :, dh:] = jnp.ones((heads, CAP * BLK, LANES), jnp.bfloat16)
    vh[:, :, dh:] = jnp.ones((heads, toks, LANES), jnp.bfloat16)

    def fill_bias(src, _):
        lists, found = slots(me, src)
        for k in range(CAP):
            hit = jnp.max(jnp.where(lists == found[k], 1, 0), axis=1, keepdims=True)
            bias[src, :, k * BLK:(k + 1) * BLK] = jnp.broadcast_to(
                jnp.where(hit > 0, 0.0, MASKED), (own, BLK))
        return 0

    lax.fori_loop(0, me + 1, fill_bias, 0)

    load_q.wait()

    def spread_q(b, _):
        at = pl.ds(pl.multiple_of(b * BLK, BLK), BLK)

        def put(h, x):
            qh[h, at, :] = x

        spread(q_raw[at], put)
        return 0

    lax.fori_loop(0, own, spread_q, 0)
    load_loc.wait()
    swap.wait_recv()

    def spread_kv(b, _):
        at = pl.ds(pl.multiple_of(b * BLK, BLK), BLK)

        def put_k(h, x):
            kh[h, at, :] = x

        def put_v(h, x):
            vh[h, at, :dh] = x

        spread(loc[0, b], put_k)
        spread(loc[1, b], put_v)
        return 0

    lax.fori_loop(0, own, spread_kv, 0)

    span = min(WB * BLK, toks)

    def near(c, _):
        rows = pl.ds(pl.multiple_of(c * BLK, BLK), BLK)
        low = pl.multiple_of(jnp.maximum(c - (WB - 1), 0) * BLK, BLK)
        keys = pl.ds(low, span)
        key_pos = low + lax.broadcasted_iota(jnp.int32, (BLK, span), 1)
        query_pos = c * BLK + lax.broadcasted_iota(jnp.int32, (BLK, span), 0)
        seen = key_pos <= query_pos
        for h in range(heads):
            s = lax.dot_general(qh[h, rows, :], kh[h, keys, :], NT,
                                preferred_element_type=jnp.float32) * SCALE
            s = jnp.where(seen, s, MASKED)
            m = jnp.max(s, axis=1, keepdims=True)
            p = jnp.exp2(s - m).astype(jnp.bfloat16)
            acc[h, rows, :] = jnp.dot(p, vh[h, keys, :], preferred_element_type=jnp.float32)
            top[h, rows, :] = jnp.broadcast_to(m, (BLK, LANES))
        return 0

    lax.fori_loop(0, own, near, 0)

    def merge(h, rows, k, v, row_bias):
        s = lax.dot_general(qh[h, rows, :], k, NT, preferred_element_type=jnp.float32) * SCALE
        if row_bias is not None:
            s = s + row_bias
        old = top[h, rows, :]
        m = jnp.maximum(old, jnp.max(s, axis=1, keepdims=True))
        wide = jnp.concatenate([m] * (s.shape[1] // LANES), axis=1)
        p = jnp.exp2(s - wide).astype(jnp.bfloat16)
        a = jnp.exp2(old - m)
        acc[h, rows, :] = acc[h, rows, :] * jnp.concatenate([a, a], axis=1) + jnp.dot(
            p, v, preferred_element_type=jnp.float32)
        top[h, rows, :] = m

    def spread_pair(get):
        for k in range(CAP):
            at = slice(k * BLK, (k + 1) * BLK)

            def put_k(h, x):
                tk[h, at, :] = x

            def put_v(h, x):
                tv[h, at, :dh] = x

            spread(get(0, k), put_k)
            spread(get(1, k), put_v)

    def far_all(src):
        def one(c, _):
            rows = pl.ds(pl.multiple_of(c * BLK, BLK), BLK)
            row_bias = bias[src, pl.ds(c, 1), :]
            for h in range(heads):
                merge(h, rows, tk[h], tv[h], row_bias)
            return 0

        lax.fori_loop(0, own, one, 0)

    _, found = slots(me, me)
    at_mine = [local_row(b) for b in found]
    spread_pair(lambda kind, k: loc[kind, at_mine[k]])
    far_all(me)

    @pl.when(me > 0)
    def _():
        rim_copy(1, ahead).wait_recv()
        rim_pass(1).start()

    def far_step(i, _):
        src = me - 1 - i
        far_arrival(src).wait_recv()
        far_pass(src).start()
        far_pass(src).wait_recv()
        spread_pair(lambda kind, k: far[kind, src, k])
        far_all(src)
        return 0

    lax.fori_loop(0, me, far_step, 0)

    def finish(c, _):
        rows = pl.ds(pl.multiple_of(c * BLK, BLK), BLK)
        for h in range(heads):
            scr[pl.ds(h, BLK, stride=heads), :] = acc[h, rows, :dh] / acc[h, rows, dh:]
        o_raw[rows] = scr[...].reshape(BLK, heads, dh).astype(jnp.bfloat16)
        pltpu.make_async_copy(o_raw.at[rows], out.at[rows], out_sem.at[c]).start()
        return 0

    lax.fori_loop(min(rims, own), own, finish, 0)

    for j in range(1, WB):
        @pl.when(me > 0)
        def _():
            if j > 1:
                rim_copy(j, ahead).wait_recv()
                rim_pass(j).start()
            rim_pass(j).wait_recv()

            def put_k(h, x):
                tk[h, :BLK, :] = x

            def put_v(h, x):
                tv[h, :BLK, :dh] = x

            spread(rim[0, j - 1], put_k)
            spread(rim[1, j - 1], put_v)

            def one(c, _):
                rows = pl.ds(pl.multiple_of(c * BLK, BLK), BLK)
                for h in range(heads):
                    merge(h, rows, tk[h, :BLK, :], tv[h, :BLK, :], None)
                return 0

            lax.fori_loop(0, min(WB - j, own), one, 0)

        if WB - j - 1 < own:
            finish(WB - j - 1, 0)

    def drain(c, _):
        rows = pl.ds(pl.multiple_of(c * BLK, BLK), BLK)
        pltpu.make_async_copy(o_raw.at[rows], out.at[rows], out_sem.at[c]).wait()
        return 0

    lax.fori_loop(0, own, drain, 0)
    swap.wait_send()

    @pl.when(has_next)
    def _():
        for j in range(1, WB):
            rim_copy(j, ahead).wait_send()

    @pl.when(me > 0)
    def _():
        for j in range(1, WB):
            rim_pass(j).wait_send()

    def sent(i, _):
        far_copy(spans - 1 - i).wait_send()
        return 0

    lax.fori_loop(0, later, sent, 0)

    def passed(src, _):
        far_pass(src).wait_send()
        return 0

    lax.fori_loop(0, me, passed, 0)


def local(spans, queries, keys_values, far_list, far_count):
    toks, heads, members, dh = queries.shape
    own = toks // BLK
    rims = WB - 1
    slot = jnp.arange(far_list.shape[1], dtype=jnp.int32)
    listed = jnp.where(slot[None, :] < far_count[:, None], far_list, -1)
    bf16, f32 = jnp.bfloat16, jnp.float32
    hbm = pl.BlockSpec(memory_space=pl.ANY)
    dma = pltpu.SemaphoreType.DMA
    result = pl.pallas_call(
        functools.partial(kernel, spans),
        out_shape=jax.ShapeDtypeStruct((toks, heads, dh), bf16),
        in_specs=[pl.BlockSpec(memory_space=pltpu.VMEM), hbm, hbm],
        out_specs=hbm,
        scratch_shapes=[
            pltpu.VMEM((toks, heads, dh), bf16),
            pltpu.VMEM((own, BLK, heads, dh), bf16),
            pltpu.VMEM((2, own, BLK, heads, dh), bf16),
            pltpu.VMEM((2, rims, BLK, heads, dh), bf16),
            pltpu.VMEM((2, spans, CAP, BLK, heads, dh), bf16),
            pltpu.VMEM((spans, CAP, BLK, heads, dh), bf16),
            pltpu.VMEM((heads, toks, dh), bf16),
            pltpu.VMEM((heads, toks, dh), bf16),
            pltpu.VMEM((heads, toks, dh + LANES), bf16),
            pltpu.VMEM((heads, CAP * BLK, dh), bf16),
            pltpu.VMEM((heads, CAP * BLK, dh + LANES), bf16),
            pltpu.VMEM((heads, toks, dh + LANES), f32),
            pltpu.VMEM((heads, toks, LANES), f32),
            pltpu.VMEM((spans, own, CAP * BLK), f32),
            pltpu.VMEM((BLK * heads, dh), f32),
            pltpu.VMEM((toks, heads, dh), bf16),
            dma((3,)), dma, dma,
            dma((rims,)), dma((rims,)), dma((rims,)), dma((rims,)),
            dma((spans,)), dma((spans,)), dma((spans,)), dma((spans,)),
            dma((own,)),
        ],
        compiler_params=pltpu.CompilerParams(
            collective_id=0, has_side_effects=True, vmem_limit_bytes=62 << 20),
    )(listed, queries.reshape(toks, heads, dh), keys_values.reshape(-1, own, BLK, heads, dh))
    return result.reshape(queries.shape)


def solution(mesh):
    in_specs = (
        P(("groups", "ctx"), "head", "rep", None),
        P("rep", ("groups", "ctx"), "head", None),
        P("groups", None),
        P("groups"),
    )
    out_specs = P(("groups", "ctx"), "head", "rep", None)
    return jax.shard_map(
        functools.partial(local, mesh.shape["ctx"]),
        mesh=mesh, in_specs=in_specs, out_specs=out_specs, check_vma=False)
```

time: 361 us -> 93.9 us (0.26); the launches traced: 354 us -> 92.7 us
  matrix products: 126 us -> 0 us
  other arithmetic: 120 us -> 1.33 us
  Pallas kernels: 0 us -> 87.6 us
  local copies, waits for them, and re-layouts: 79.4 us -> 3.81 us
  waiting for transfers between devices: 11.4 us -> 0 us
  starting transfers between devices: 9.94 us -> 0 us
  loops' own time: 7.96 us -> 0 us
    dot_general x8 -> x0, matrix products: 126 us -> none  [the longest x2 45.4 us: far_group(): jnp.einsum('bhgqk,bkhd->bhgqd', weights.astype(jnp.bfloat16), value_tile,...]
    pallas_call x0 -> x1, Pallas kernels: none -> 87.6 us  [local(): pl.pallas_call(functools.partial(kernel, spans), out_shape=jax.ShapeDtype...]
    select_n x9 -> x1, other arithmetic: 53.9 us -> 1.33 us  [local(): listed = jnp.where(slot[None, :] < far_count[:, None], far_list, -1)]
    reduce_sum x6 -> x0, other arithmetic: 47.8 us -> none  [the longest x4 47.6 us: group_weights(): return (summit, weights, jnp.sum(weights, axis=-1, keepdims=True))]
    gather x5 -> x0, local copies, waits for them, and re-layouts: 37.5 us -> none  [the longest x2 17.7 us: far_group(): jnp.take(pool_pair[1], slot_tile.reshape(-1), axis=0)]
    ppermute x2 -> x0, waiting for transfers between devices: 11.4 us -> none  [the longest x1 11.4 us: from_behind(): return lax.ppermute(x, axis, pairs)]
    concatenate x3 -> x0, other arithmetic: 8.22 us -> none  [the longest x1 4.91 us: local(): extended = jnp.concatenate([rim_pair, local_pair], axis=1)]
    another operation x2 -> x0, loops' own time: 7.96 us -> none  [the longest x1 7.85 us: local(): near_top, near_out, near_sum = lax.map(near_part, starts)]
  transfers between devices with their start and end apart: 3 -> 0, of which waited for: 1 -> 0; matrix products, arithmetic and copies ran while one was open for 28% -> 0% of each run, Pallas kernels for 0% -> 0%
where the time goes in v1:
time: 93.9 us; the launch traced here: 92.7 us
  Pallas kernels  87.6 us (93%)
  local copies, waits for them, and re-layouts  3.81 us (4%)
  other arithmetic  1.33 us (1%)
    pallas_call x1, Pallas kernels, local(): pl.pallas_call(functools.partial(kernel, spans), out_shape=jax.ShapeDtype...  87.6 us
    unnamed x2, local copies, waits for them, and re-layouts  3.81 us

profile of v1, /device:TPU:17, one launch (start us, length us, event | category | flops | bytes accessed | tf_op | source)
XLA Modules:
  0.0 92.7 jit_solution(14823474366679791361)
XLA Ops:
  0.0 0.8 copy.5
  0.8 1.3 %fusion.listed = s32[32,16]{1,0:T(8,128)} fusion(s32[32,16]{1,0:T(8,128)S(1)} %copy.5, s32[32]{0:T(128)} %param.7), kind=kLoop, calls=%fused_computation.1 | loop fusion | flops 1024 | bytes 4224 | tf_op jit(solution)/shard_map/jit(_where)/select_n | solution.py:337
  2.1 87.6 %shard_map.46 = bf16[1024,8,128]{2,1,0:T(8,128)(2,1)} custom-call(s32[32,16]{1,0:T(8,128)} %fusion.listed, bf16[1024,8,128]{2,1,0:T(8,128)(2,1)} %bitcast.6, bf16[1,8,128,8,128]{4,3,2,1,0:T(8,128)(2,1)} %bitcast.7), custom_call_target="tpu_custom_call" | custom-call | tf_op jit(solution)/shard_map/pallas_call | solution.py:341
  89.7 3.0 %copy.8 = bf16[1024,8,1,128]{3,1,2,0:T(8,128)(2,1)} copy(bf16[1024,8,1,128]{3,1,2,0:T(8,128)(2,1)} %bitcast.5) | data formatting | bytes 4194304

commit v2 on v1

v2 whole, which is shorter than its diff:
```python
import functools
import math

import jax
import jax.numpy as jnp
from jax import lax
from jax.experimental import pallas as pl
from jax.experimental.pallas import tpu as pltpu
from jax.sharding import PartitionSpec as P

BLK = 128
WB = 4
FSEL = 16
CAP = 2

LANES = 128
MASKED = -1e30
SCALE = math.log2(math.e) / 12.0
NT = (((1,), (1,)), ((), ()))


def kernel(
    spans, lists_in, counts, q_in, kv_in, out,
    q_raw, raw, mine, loc, rim_raw, rim, far, sendbuf, qh, tk, tv, acc, top, bias, scr, o_raw,
    in_sem, x_send, x_recv, rz_send, rz_recv, rf_send, rf_recv,
    fz_send, fz_recv, ff_send, ff_recv, out_sem,
):
    toks, heads, dh = q_in.shape
    own = toks // BLK
    me = lax.axis_index("ctx")
    side = lax.axis_index("rep")
    mate = {"rep": 1 - side}
    rims = WB - 1

    load_kv = pltpu.make_async_copy(kv_in.at[0], raw, in_sem.at[0])
    load_q = pltpu.make_async_copy(q_in, q_raw, in_sem.at[1])
    load_kv.start()
    load_q.start()

    barrier = pltpu.get_barrier_semaphore()
    pl.semaphore_signal(barrier, inc=1, device_id=mate)

    def greet(i, _):
        pl.semaphore_signal(barrier, inc=1, device_id={"ctx": lax.rem(me + i, spans)})
        return 0

    lax.fori_loop(1, spans, greet, 0)
    pl.semaphore_wait(barrier, spans)

    def rim_copy(j, to):
        return pltpu.make_async_remote_copy(
            src_ref=kv_in.at[0, own - j] if j == 1 else mine.at[own - j],
            dst_ref=rim_raw.at[side] if j == 1 else rim.at[side, j - 2],
            send_sem=rz_send.at[j - 1], recv_sem=rz_recv.at[j - 1],
            device_id={"ctx": to},
        )

    def rim_pass(j):
        return pltpu.make_async_remote_copy(
            src_ref=rim_raw.at[side] if j == 1 else rim.at[side, j - 2],
            dst_ref=rim_raw.at[side] if j == 1 else rim.at[side, j - 2],
            send_sem=rf_send.at[j - 1], recv_sem=rf_recv.at[j - 1],
            device_id=mate,
        )

    def far_copy(to):
        return pltpu.make_async_remote_copy(
            src_ref=sendbuf.at[to], dst_ref=far.at[side, me],
            send_sem=fz_send.at[to], recv_sem=fz_recv.at[me],
            device_id={"ctx": to},
        )

    def far_arrival(src):
        return pltpu.make_async_remote_copy(
            src_ref=sendbuf.at[src], dst_ref=far.at[side, src],
            send_sem=fz_send.at[src], recv_sem=fz_recv.at[src],
            device_id={"ctx": src},
        )

    def far_pass(src):
        return pltpu.make_async_remote_copy(
            src_ref=far.at[side, src], dst_ref=far.at[side, src],
            send_sem=ff_send.at[src], recv_sem=ff_recv.at[src],
            device_id=mate,
        )

    ahead = lax.rem(me + 1, spans)
    has_next = me + 1 < spans

    @pl.when(has_next)
    def _():
        rim_copy(1, ahead).start()

    def spread(part, block, put):
        scr[part] = block.astype(jnp.float32).reshape(BLK * heads, dh)
        for h in range(heads):
            put(h, scr[part, pl.ds(h, BLK, stride=heads), :].astype(jnp.bfloat16))

    load_kv.wait()
    parts = scr.shape[0]

    def spread_mine(i, _):
        for part in range(parts):
            b = i * parts + part

            def put(h, x):
                mine[b, h] = x
                loc[side, b, h] = x

            spread(part, raw[b], put)
        return 0

    lax.fori_loop(0, own // parts, spread_mine, 0)

    swap = pltpu.make_async_remote_copy(
        src_ref=mine, dst_ref=loc.at[side],
        send_sem=x_send, recv_sem=x_recv, device_id=mate,
    )
    swap.start()

    big = jnp.int32(1 << 30)
    slot = lax.broadcasted_iota(jnp.int32, lists_in.shape, 0)
    block_of = lax.broadcasted_iota(jnp.int32, lists_in.shape, 1)
    listed = jnp.where(slot < counts[...], lists_in[...], -1)

    def slots(dst, src):
        inside = ((listed >= src * own) & (listed < src * own + own)
                  & (block_of >= dst * own) & (block_of < dst * own + own))
        first = jnp.min(jnp.where(inside, listed, big))
        second = jnp.min(jnp.where(inside & (listed > first), listed, big))
        return first, second

    def local_row(block):
        row = jnp.where(block < big, block - me * own, 0)
        return jnp.clip(row, 0, own - 1)

    def fill(i, _):
        to = spans - 1 - i
        found = slots(to, me)
        for k in range(CAP):
            sendbuf[to, k] = mine[local_row(found[k])]
        return 0

    later = spans - 1 - me
    lax.fori_loop(0, later, fill, 0)

    def push(i, _):
        far_copy(spans - 1 - i).start()
        return 0

    lax.fori_loop(0, later, push, 0)

    @pl.when(has_next)
    def _():
        for j in range(2, WB):
            rim_copy(j, ahead).start()

    ones = jnp.ones((BLK, LANES), jnp.bfloat16)

    def fill_bias(src, _):
        found = slots(me, src)
        for k in range(CAP):
            hit = jnp.max(jnp.where(listed == found[k], 1.0, 0.0), axis=0, keepdims=True)
            for c in range(own):
                mark = jnp.where(block_of[:1] == me * own + c, hit, 0.0)
                mark = jnp.max(mark, axis=1, keepdims=True)
                bias[src, c, :, k * BLK:(k + 1) * BLK] = jnp.broadcast_to(
                    jnp.where(mark > 0.5, 0.0, MASKED), (1, BLK))
        return 0

    lax.fori_loop(0, me + 1, fill_bias, 0)

    load_q.wait()

    def spread_q(i, _):
        for part in range(parts):
            at = pl.ds(pl.multiple_of((i * parts + part) * BLK, BLK), BLK)

            def put(h, x):
                qh[h, at, :] = x

            spread(part, q_raw[at], put)
        return 0

    lax.fori_loop(0, own // parts, spread_q, 0)
    swap.wait_recv()

    wide = min(WB, own)
    span = wide * BLK

    def near(c, _):
        rows = pl.ds(pl.multiple_of(c * BLK, BLK), BLK)
        low = jnp.maximum(c - (WB - 1), 0)
        keys = pl.ds(low, wide)
        key_pos = low * BLK + lax.broadcasted_iota(jnp.int32, (BLK, span), 1)
        query_pos = c * BLK + lax.broadcasted_iota(jnp.int32, (BLK, span), 0)
        seen = key_pos <= query_pos
        for h in range(heads):
            s = lax.dot_general(qh[h, rows, :], loc[0, keys, h].reshape(span, dh), NT,
                                preferred_element_type=jnp.float32) * SCALE
            s = jnp.where(seen, s, MASKED)
            m = jnp.max(s, axis=1, keepdims=True)
            p = jnp.exp2(s - m).astype(jnp.bfloat16)
            v = jnp.concatenate([loc[1, keys, h].reshape(span, dh)] + [jnp.ones((span, LANES), jnp.bfloat16)], axis=1)
            acc[h, rows, :] = jnp.dot(p, v, preferred_element_type=jnp.float32)
            top[h, rows, :] = jnp.broadcast_to(m, (BLK, LANES))
        return 0

    lax.fori_loop(0, own, near, 0)

    def merge(h, rows, k, v, row_bias):
        s = lax.dot_general(qh[h, rows, :], k, NT, preferred_element_type=jnp.float32) * SCALE
        if row_bias is not None:
            s = s + row_bias
        old = top[h, rows, :]
        m = jnp.maximum(old, jnp.max(s, axis=1, keepdims=True))
        spread_m = jnp.concatenate([m] * (s.shape[1] // LANES), axis=1)
        p = jnp.exp2(s - spread_m).astype(jnp.bfloat16)
        a = jnp.exp2(old - m)
        acc[h, rows, :] = acc[h, rows, :] * jnp.concatenate([a, a], axis=1) + jnp.dot(
            p, v, preferred_element_type=jnp.float32)
        top[h, rows, :] = m

    def stack(get, h):
        k = jnp.concatenate([get(0, n, h) for n in range(CAP)], axis=0)
        v = jnp.concatenate(
            [jnp.concatenate([get(1, n, h), ones], axis=1) for n in range(CAP)], axis=0)
        return k, v

    def far_all(src, get):
        def one(c, _):
            rows = pl.ds(pl.multiple_of(c * BLK, BLK), BLK)
            row_bias = bias[src, c]
            for h in range(heads):
                merge(h, rows, *stack(get, h), row_bias)
            return 0

        lax.fori_loop(0, own, one, 0)

    found_mine = slots(me, me)
    at_mine = [local_row(b) for b in found_mine]
    far_all(me, lambda kind, k, h: loc[kind, at_mine[k], h])

    def rim_all(j, get):
        def one(c, _):
            rows = pl.ds(pl.multiple_of(c * BLK, BLK), BLK)
            for h in range(heads):
                merge(h, rows, get(0, h), jnp.concatenate([get(1, h), ones], axis=1), None)
            return 0

        lax.fori_loop(0, min(WB - j, own), one, 0)

    @pl.when(me > 0)
    def _():
        rim_copy(1, ahead).wait_recv()
        rim_pass(1).start()
        rim_pass(1).wait_recv()

        def put_k(h, x):
            tk[h] = x

        def put_v(h, x):
            tv[h] = x

        spread(0, rim_raw[0], put_k)
        spread(1, rim_raw[1], put_v)
        rim_all(1, lambda kind, h: (tv if kind else tk)[h])

    def far_step(src, _):
        far_arrival(src).wait_recv()
        far_pass(src).start()
        far_pass(src).wait_recv()
        far_all(src, lambda kind, k, h: far[kind, src, k, h])
        return 0

    lax.fori_loop(0, me, far_step, 0)

    def finish(c, _):
        rows = pl.ds(pl.multiple_of(c * BLK, BLK), BLK)
        part = lax.rem(c, parts)
        for h in range(heads):
            scr[part, pl.ds(h, BLK, stride=heads), :] = acc[h, rows, :dh] / acc[h, rows, dh:]
        o_raw[rows] = scr[part].reshape(BLK, heads, dh).astype(jnp.bfloat16)
        pltpu.make_async_copy(o_raw.at[rows], out.at[rows], out_sem.at[c]).start()
        return 0

    lax.fori_loop(min(rims - 1, own), own, finish, 0)

    for j in range(2, WB):
        @pl.when(me > 0)
        def _():
            rim_copy(j, ahead).wait_recv()
            rim_pass(j).start()
            rim_pass(j).wait_recv()
            rim_all(j, lambda kind, h: rim[kind, j - 2, h])

        if WB - j - 1 < own:
            finish(WB - j - 1, 0)

    def drain(c, _):
        rows = pl.ds(pl.multiple_of(c * BLK, BLK), BLK)
        pltpu.make_async_copy(o_raw.at[rows], out.at[rows], out_sem.at[c]).wait()
        return 0

    lax.fori_loop(0, own, drain, 0)
    swap.wait_send()

    @pl.when(has_next)
    def _():
        for j in range(1, WB):
            rim_copy(j, ahead).wait_send()

    @pl.when(me > 0)
    def _():
        for j in range(1, WB):
            rim_pass(j).wait_send()

    def sent(i, _):
        far_copy(spans - 1 - i).wait_send()
        return 0

    lax.fori_loop(0, later, sent, 0)

    def passed(src, _):
        far_pass(src).wait_send()
        return 0

    lax.fori_loop(0, me, passed, 0)


def local(spans, queries, keys_values, far_list, far_count):
    toks, heads, members, dh = queries.shape
    own = toks // BLK
    rims = WB - 1
    bf16, f32 = jnp.bfloat16, jnp.float32
    hbm = pl.BlockSpec(memory_space=pl.ANY)
    dma = pltpu.SemaphoreType.DMA
    result = pl.pallas_call(
        functools.partial(kernel, spans),
        out_shape=jax.ShapeDtypeStruct((toks, heads, dh), bf16),
        in_specs=[pl.BlockSpec(memory_space=pltpu.VMEM)] * 2 + [hbm, hbm],
        out_specs=hbm,
        scratch_shapes=[
            pltpu.VMEM((toks, heads, dh), bf16),
            pltpu.VMEM((own, BLK, heads, dh), bf16),
            pltpu.VMEM((own, heads, BLK, dh), bf16),
            pltpu.VMEM((2, own, heads, BLK, dh), bf16),
            pltpu.VMEM((2, BLK, heads, dh), bf16),
            pltpu.VMEM((2, rims - 1, heads, BLK, dh), bf16),
            pltpu.VMEM((2, spans, CAP, heads, BLK, dh), bf16),
            pltpu.VMEM((spans, CAP, heads, BLK, dh), bf16),
            pltpu.VMEM((heads, toks, dh), bf16),
            pltpu.VMEM((heads, BLK, dh), bf16),
            pltpu.VMEM((heads, BLK, dh), bf16),
            pltpu.VMEM((heads, toks, dh + LANES), f32),
            pltpu.VMEM((heads, toks, LANES), f32),
            pltpu.VMEM((spans, own, 1, CAP * BLK), f32),
            pltpu.VMEM((2, BLK * heads, dh), f32),
            pltpu.VMEM((toks, heads, dh), bf16),
            dma((2,)), dma, dma,
            dma((rims,)), dma((rims,)), dma((rims,)), dma((rims,)),
            dma((spans,)), dma((spans,)), dma((spans,)), dma((spans,)),
            dma((own,)),
        ],
        compiler_params=pltpu.CompilerParams(
            collective_id=0, has_side_effects=True, vmem_limit_bytes=62 << 20),
    )(far_list.T, far_count.reshape(1, -1), queries.reshape(toks, heads, dh), keys_values.reshape(-1, own, BLK, heads, dh))
    return result.reshape(queries.shape)


def solution(mesh):
    in_specs = (
        P(("groups", "ctx"), "head", "rep", None),
        P("rep", ("groups", "ctx"), "head", None),
        P("groups", None),
        P("groups"),
    )
    out_specs = P(("groups", "ctx"), "head", "rep", None)
    return jax.shard_map(
        functools.partial(local, mesh.shape["ctx"]),
        mesh=mesh, in_specs=in_specs, out_specs=out_specs, check_vma=False)
```

time: 93.9 us -> 77.7 us (0.83); the launches traced: 92.7 us -> 77.5 us
  Pallas kernels: 87.6 us -> 74.4 us
  other arithmetic: 1.33 us -> 0 us
    pallas_call x1, Pallas kernels: 87.6 us -> 74.4 us  [local(): pl.pallas_call(functools.partial(kernel, spans), out_shape=jax.ShapeDtype...]
    select_n x1 -> x0, other arithmetic: 1.33 us -> none  [local(): listed = jnp.where(slot[None, :] < far_count[:, None], far_list, -1)]
    unnamed x2 -> x1, local copies, waits for them, and re-layouts: 3.81 us -> 3.05 us
where the time goes in v2:
time: 77.7 us; the launch traced here: 77.5 us
  Pallas kernels  74.4 us (96%)
  local copies, waits for them, and re-layouts  3.05 us (4%)
    pallas_call x1, Pallas kernels, local(): pl.pallas_call(functools.partial(kernel, spans), out_shape=jax.ShapeDtype...  74.4 us
    unnamed x1, local copies, waits for them, and re-layouts  3.05 us

profile of v2, /device:TPU:17, one launch (start us, length us, event | category | flops | bytes accessed | tf_op | source)
XLA Modules:
  0.0 77.5 jit_solution(12283625841899619752)
XLA Ops:
  0.0 74.4 %shard_map.46 = bf16[1024,8,128]{2,1,0:T(8,128)(2,1)} custom-call(s32[16,32]{1,0:T(8,128)} %bitcast.10, s32[1,32]{1,0:T(1,128)} %bitcast.11, bf16[1024,8,128]{2,1,0:T(8,128)(2,1)} %bitcast.8, bf16[1,8,128,8,128]{4,3,2,1,0:T(8,128)(2,1)} %bitcast.9), custom_call_target="tpu_custom_call" | custom-call | tf_op jit(solution)/shard_map/pallas_call | solution.py:338
  74.4 3.0 %copy.7 = bf16[1024,8,1,128]{3,1,2,0:T(8,128)(2,1)} copy(bf16[1024,8,1,128]{3,1,2,0:T(8,128)(2,1)} %bitcast.7) | data formatting | bytes 4194304

commit v3 on v2

--- a/solution.py
+++ b/solution.py
@@ -21,7 +21,7 @@
 
 def kernel(
     spans, lists_in, counts, q_in, kv_in, out,
-    q_raw, raw, mine, loc, rim_raw, rim, far, sendbuf, qh, tk, tv, acc, top, bias, scr, o_raw,
+    q_raw, raw, mine, loc, rim_raw, rim, far, sendbuf, qh, acc, top, bias, scr, o_raw,
     in_sem, x_send, x_recv, rz_send, rz_recv, rf_send, rf_recv,
     fz_send, fz_recv, ff_send, ff_recv, out_sem,
 ):
@@ -47,18 +47,30 @@
     lax.fori_loop(1, spans, greet, 0)
     pl.semaphore_wait(barrier, spans)
 
+    def raw_copy(to):
+        return pltpu.make_async_remote_copy(
+            src_ref=kv_in.at[0, own - 1], dst_ref=rim_raw.at[side],
+            send_sem=rz_send.at[0], recv_sem=rz_recv.at[0], device_id={"ctx": to},
+        )
+
+    def raw_pass():
+        return pltpu.make_async_remote_copy(
+            src_ref=rim_raw.at[side], dst_ref=rim_raw.at[side],
+            send_sem=rf_send.at[0], recv_sem=rf_recv.at[0], device_id=mate,
+        )
+
     def rim_copy(j, to):
         return pltpu.make_async_remote_copy(
-            src_ref=kv_in.at[0, own - j] if j == 1 else mine.at[own - j],
-            dst_ref=rim_raw.at[side] if j == 1 else rim.at[side, j - 2],
+            src_ref=mine.at[own - j],
+            dst_ref=rim.at[side, j - 1],
             send_sem=rz_send.at[j - 1], recv_sem=rz_recv.at[j - 1],
             device_id={"ctx": to},
         )
 
     def rim_pass(j):
         return pltpu.make_async_remote_copy(
-            src_ref=rim_raw.at[side] if j == 1 else rim.at[side, j - 2],
-            dst_ref=rim_raw.at[side] if j == 1 else rim.at[side, j - 2],
+            src_ref=rim.at[side, j - 1],
+            dst_ref=rim.at[side, j - 1],
             send_sem=rf_send.at[j - 1], recv_sem=rf_recv.at[j - 1],
             device_id=mate,
         )
@@ -89,7 +101,7 @@
 
     @pl.when(has_next)
     def _():
-        rim_copy(1, ahead).start()
+        raw_copy(ahead).start()
 
     def spread(part, block, put):
         scr[part] = block.astype(jnp.float32).reshape(BLK * heads, dh)
@@ -210,8 +222,7 @@
 
     def merge(h, rows, k, v, row_bias):
         s = lax.dot_general(qh[h, rows, :], k, NT, preferred_element_type=jnp.float32) * SCALE
-        if row_bias is not None:
-            s = s + row_bias
+        s = s + row_bias
         old = top[h, rows, :]
         m = jnp.maximum(old, jnp.max(s, axis=1, keepdims=True))
         spread_m = jnp.concatenate([m] * (s.shape[1] // LANES), axis=1)
@@ -241,30 +252,20 @@
     at_mine = [local_row(b) for b in found_mine]
     far_all(me, lambda kind, k, h: loc[kind, at_mine[k], h])
 
-    def rim_all(j, get):
-        def one(c, _):
-            rows = pl.ds(pl.multiple_of(c * BLK, BLK), BLK)
-            for h in range(heads):
-                merge(h, rows, get(0, h), jnp.concatenate([get(1, h), ones], axis=1), None)
-            return 0
-
-        lax.fori_loop(0, min(WB - j, own), one, 0)
-
     @pl.when(me > 0)
     def _():
-        rim_copy(1, ahead).wait_recv()
-        rim_pass(1).start()
-        rim_pass(1).wait_recv()
+        raw_copy(ahead).wait_recv()
+        raw_pass().start()
+        raw_pass().wait_recv()
 
         def put_k(h, x):
-            tk[h] = x
+            rim[0, 0, h] = x
 
         def put_v(h, x):
-            tv[h] = x
+            rim[1, 0, h] = x
 
         spread(0, rim_raw[0], put_k)
         spread(1, rim_raw[1], put_v)
-        rim_all(1, lambda kind, h: (tv if kind else tk)[h])
 
     def far_step(src, _):
         far_arrival(src).wait_recv()
@@ -284,18 +285,32 @@
         pltpu.make_async_copy(o_raw.at[rows], out.at[rows], out_sem.at[c]).start()
         return 0
 
-    lax.fori_loop(min(rims - 1, own), own, finish, 0)
-
-    for j in range(2, WB):
-        @pl.when(me > 0)
+    lane = lax.broadcasted_iota(jnp.int32, (1, CAP * BLK), 1)
+    once = jnp.where(lane < BLK, 0.0, MASKED)
+
+    def close(i, _):
+        last = own - 1 - i
+        j = WB - 1 - last
+
+        @pl.when((me > 0) & (j > 1))
         def _():
             rim_copy(j, ahead).wait_recv()
             rim_pass(j).start()
             rim_pass(j).wait_recv()
-            rim_all(j, lambda kind, h: rim[kind, j - 2, h])
-
-        if WB - j - 1 < own:
-            finish(WB - j - 1, 0)
+
+        def one(c, _):
+            rows = pl.ds(pl.multiple_of(c * BLK, BLK), BLK)
+            for h in range(heads):
+                merge(h, rows, *stack(lambda kind, n, h: rim[kind, j - 1, h], h), once)
+            return 0
+
+        @pl.when((me > 0) & (j > 0))
+        def _():
+            lax.fori_loop(0, last + 1, one, 0)
+
+        return finish(last, 0)
+
+    lax.fori_loop(0, own, close, 0)
 
     def drain(c, _):
         rows = pl.ds(pl.multiple_of(c * BLK, BLK), BLK)
@@ -307,12 +322,14 @@
 
     @pl.when(has_next)
     def _():
-        for j in range(1, WB):
+        raw_copy(ahead).wait_send()
+        for j in range(2, WB):
             rim_copy(j, ahead).wait_send()
 
     @pl.when(me > 0)
     def _():
-        for j in range(1, WB):
+        raw_pass().wait_send()
+        for j in range(2, WB):
             rim_pass(j).wait_send()
 
     def sent(i, _):
@@ -346,12 +363,10 @@
             pltpu.VMEM((own, heads, BLK, dh), bf16),
             pltpu.VMEM((2, own, heads, BLK, dh), bf16),
             pltpu.VMEM((2, BLK, heads, dh), bf16),
-            pltpu.VMEM((2, rims - 1, heads, BLK, dh), bf16),
+            pltpu.VMEM((2, rims, heads, BLK, dh), bf16),
             pltpu.VMEM((2, spans, CAP, heads, BLK, dh), bf16),
             pltpu.VMEM((spans, CAP, heads, BLK, dh), bf16),
             pltpu.VMEM((heads, toks, dh), bf16),
-            pltpu.VMEM((heads, BLK, dh), bf16),
-            pltpu.VMEM((heads, BLK, dh), bf16),
             pltpu.VMEM((heads, toks, dh + LANES), f32),
             pltpu.VMEM((heads, toks, LANES), f32),
             pltpu.VMEM((spans, own, 1, CAP * BLK), f32),

time: 77.7 us -> 75.5 us (0.972)
  Pallas kernels: 74.4 us -> 72.3 us
    pallas_call x1, Pallas kernels: 74.4 us -> 72.3 us  [local(): pl.pallas_call(functools.partial(kernel, spans), out_shape=jax.ShapeDtype...]
where the time goes in v3:
time: 75.5 us; the launch traced here: 75.3 us
  Pallas kernels  72.3 us (96%)
  local copies, waits for them, and re-layouts  3.05 us (4%)
    pallas_call x1, Pallas kernels, local(): pl.pallas_call(functools.partial(kernel, spans), out_shape=jax.ShapeDtype...  72.3 us
    unnamed x1, local copies, waits for them, and re-layouts  3.05 us

profile of v3, /device:TPU:17, one launch (start us, length us, event | category | flops | bytes accessed | tf_op | source)
XLA Modules:
  0.0 75.3 jit_solution(7797391060619877532)
XLA Ops:
  0.0 72.3 %shard_map.46 = bf16[1024,8,128]{2,1,0:T(8,128)(2,1)} custom-call(s32[16,32]{1,0:T(8,128)} %bitcast.10, s32[1,32]{1,0:T(1,128)} %bitcast.11, bf16[1024,8,128]{2,1,0:T(8,128)(2,1)} %bitcast.8, bf16[1,8,128,8,128]{4,3,2,1,0:T(8,128)(2,1)} %bitcast.9), custom_call_target="tpu_custom_call" | custom-call | tf_op jit(solution)/shard_map/pallas_call | solution.py:355
  72.3 3.0 %copy.7 = bf16[1024,8,1,128]{3,1,2,0:T(8,128)(2,1)} copy(bf16[1024,8,1,128]{3,1,2,0:T(8,128)(2,1)} %bitcast.7) | data formatting | bytes 4194304
